TPU v7x, 32 devices: a whole 2x2x4 slice. The times are simulated.
32 devices in a mesh: angle: 8 (over z, x), row: 4 (over y, core).
Axes of the slice: x: 2, y: 2, z: 4, core: 2. Of those that a mesh axis runs over, the one named last changes fastest.
Arguments:
- raw_frames: bfloat16 [8, 8, 32, 2048], P('angle', None, 'row'), may hold values from 0.5 to 1.5
- step_index: int32 [8, 8], P('angle'), may hold values from 0 to 7, each once within a row
- partner: int32 [8], replicated, may hold values from 0 to 7, as said below
- flat_field: bfloat16 [2, 32, 2048], P(None, ('row', 'angle')), may hold values from -4 to 4
Outputs:
- filtered: bfloat16 [8, 32, 2048], P(None, ('row', 'angle'))
Inputs may be any that keep to these rules, and one draw needn't show every extreme that they name: partner[partner[a]] = a, and every angle of the first half of the 8 angles is paired with one of the second half. `step_index`: each angle's row names every phase step once.
All inputs are finite; a program needn't handle non-finite values.
Results may differ from a plain program's by a relative error of at most 0.0078.
Values may be sent and summed in bfloat16 or wider, within the bound.
A program may use at most 128 MiB of HBM per device.

v0:
```python
import math

import jax
import jax.numpy as jnp
import numpy as np
from jax import lax
from jax.sharding import PartitionSpec as P

two_pi = 2.0 * math.pi


def padded_2(block, sides, width):
    for axis, dim in sides:
        count = lax.axis_size(axis)
        forward = [(i, i + 1) for i in range(count - 1)]
        backward = [(target, source) for source, target in forward]
        low = lax.ppermute(
            lax.slice_in_dim(block, block.shape[dim] - width, None, axis=dim), axis, forward
        )
        high = lax.ppermute(lax.slice_in_dim(block, 0, width, axis=dim), axis, backward)
        block = jnp.concatenate([low, block, high], axis=dim)
    return block


def make_dpc(smooth_cos, smooth_sin, smooth_mean, flat, steps):
    flat_cos = flat[0].astype(jnp.float32)[None]
    flat_sin = flat[1].astype(jnp.float32)[None]
    value = steps * (
        smooth_sin.astype(jnp.float32) * flat_cos - smooth_cos.astype(jnp.float32) * flat_sin
    )
    return (value / smooth_mean.astype(jnp.float32)).astype(jnp.bfloat16)


def half_tables(det, padlen):
    column = np.arange(det, dtype=np.int64)[:, None]
    freq = np.arange(det, dtype=np.int64)[None, :]
    theta = (column * freq % padlen).astype(np.float32) * np.float32(two_pi / padlen)
    cos_half = np.cos(theta).astype(np.float32)
    sin_half = np.sin(theta).astype(np.float32)
    forward = np.concatenate([cos_half, sin_half], axis=1)
    backward = np.concatenate([sin_half, -cos_half], axis=1)
    parity = np.where(np.arange(det) % 2 == 0, 1.0, -1.0).astype(np.float32)
    signs = np.concatenate([parity, parity])
    return (forward, backward, signs)


def filter_rows(rows, det):
    padlen = rows.shape[1]
    forward_np, backward_np, signs_np = half_tables(det, padlen)
    forward = jnp.asarray(forward_np).astype(jnp.bfloat16)
    backward = jnp.asarray(backward_np).astype(jnp.bfloat16)
    signs = jnp.asarray(signs_np)
    left_part = jnp.dot(rows[:, :det], forward, preferred_element_type=jnp.float32)
    right_part = jnp.dot(rows[:, det:], forward, preferred_element_type=jnp.float32)
    spec = (left_part + right_part * signs[None]).astype(jnp.bfloat16)
    flipped = spec * signs[None].astype(jnp.bfloat16)
    total = lax.dot_general(
        flipped, backward, (((1,), (1,)), ((), ())), preferred_element_type=jnp.float32
    )
    return (total * (2.0 / padlen)).astype(jnp.bfloat16)


def local(raw_frames, step_index, partner, flat_field):
    ang_dev, steps, rows_blk, det = raw_frames.shape
    phase = step_index.astype(jnp.float32) * (two_pi / steps)
    weight_cos = jnp.cos(phase)
    weight_sin = jnp.sin(phase)
    corr_cos = jnp.zeros((ang_dev, rows_blk, det), jnp.float32)
    corr_sin = jnp.zeros((ang_dev, rows_blk, det), jnp.float32)
    corr_mean = jnp.zeros((ang_dev, rows_blk, det), jnp.float32)
    for step in range(steps):
        frame = raw_frames[:, step].astype(jnp.float32)
        corr_cos = corr_cos + frame * weight_cos[:, step][:, None, None]
        corr_sin = corr_sin + frame * weight_sin[:, step][:, None, None]
        corr_mean = corr_mean + frame
    stacked = jnp.stack([corr_cos, corr_sin, corr_mean])
    edges = jnp.concatenate([stacked[:, :, :1], stacked[:, :, -1:]], axis=2)
    rims = padded_2(edges, (("row", 2),), 1)
    padded = jnp.concatenate([rims[:, :, :1], stacked, rims[:, :, 3:]], axis=2)
    smoothed = (
        0.25 * padded[:, :, :-2] + 0.5 * padded[:, :, 1:-1] + 0.25 * padded[:, :, 2:]
    ).astype(jnp.bfloat16)
    flat_block = lax.all_gather(flat_field, "angle", axis=1, tiled=True)
    dpc = make_dpc(smoothed[0], smoothed[1], smoothed[2], flat_block, steps)
    dpc_all = lax.all_to_all(dpc, "angle", split_axis=1, concat_axis=0, tiled=True)
    angles_all, rows_here, _ = dpc_all.shape
    mirror = jnp.take(dpc_all, partner, axis=0)[:, :, ::-1]
    combined = jnp.concatenate([-mirror, dpc_all], axis=2)
    flat_rows = combined.reshape(angles_all * rows_here, 2 * det)
    result = filter_rows(flat_rows, det)
    return result.reshape(angles_all, rows_here, det)


def solution(mesh):
    in_specs = (
        P("angle", None, "row", None),
        P("angle", None),
        P(),
        P(None, ("row", "angle"), None),
    )
    out_specs = P(None, ("row", "angle"), None)
    return jax.shard_map(local, mesh=mesh, in_specs=in_specs, out_specs=out_specs, check_vma=False)
```

profile of v0, /device:TPU:0, one launch (start us, length us, event | category | flops | bytes accessed | tf_op | source)
XLA Modules:
  0.0 89.6 jit_solution(1640612086476328610)
XLA Ops:
  0.0 0.7 fusion.25
  0.7 0.9 fusion.27
  1.6 0.7 fusion.28
  2.3 5.4 %multiply_add_fusion = f32[1,1,8,2048]{3,0,2,1:T(1,128)S(1)} fusion(bf16[1,1,8,2048]{3,2,1,0:T(8,128)(2,1)S(1)} %get-tuple-element.16, bf16[1,1,8,2048]{3,2,1,0:T(8,128)(2,1)S(1)} %get-tuple-element.15, bf16[1,1,8,2048]{3,2,1,0:T(8,128)(2,1)S(1)} %get-tuple-element.14, bf16[1,1,8,2048]{3,2,1,0:T(8,128)(2,1)S(1)} %get-tuple-element.13, ...), kind=kLoop, calls=%fused_computation.43 | loop fusion | flops 376832 | bytes 327712 | tf_op jit(solution)/shard_map/add | solution.py:74
  7.7 5.5 %multiply_add_fusion.1 = (f32[1,1,8,2048]{3,0,2,1:T(1,128)S(1)}, f32[1,1,8,2048]{3,0,2,1:T(1,128)S(1)}) fusion(bf16[1,1,8,2048]{3,2,1,0:T(8,128)(2,1)S(1)} %get-tuple-element.16, bf16[1,1,8,2048]{3,2,1,0:T(8,128)(2,1)S(1)} %get-tuple-element.15, bf16[1,1,8,2048]{3,2,1,0:T(8,128)(2,1)S(1)} %get-tuple-element.14, ...), kind=kLoop, calls=%fused_computation.44 | loop fusion | flops 491520 | bytes 393248 | tf_op jit(solution)/shard_map/add | solution.py:73
  13.3 0.2 pad_maximum_fusion.6
  13.5 2.4 %collective-permute-start = (f32[3,1,1,2048]{3,0,2,1:T(4,128)S(1)}, f32[3,1,1,2048]{3,0,2,1:T(4,128)S(1)}, u32[]{:S(2)}, u32[]{:S(2)}) collective-permute-start(f32[3,1,1,2048]{3,0,2,1:T(4,128)S(1)} %get-tuple-element.5), channel_id=1, source_target_pairs={{0,1},{1,2},{2,3},{4,5},{5,6},{6,7},{8,9},{9,10},{10,11},{12,13},{... | collective-permute-start | bytes 73736 | tf_op jit(solution)/shard_map/ppermute | solution.py:17
  15.8 1.3 %collective-permute-start.1 = (f32[3,1,1,2048]{3,0,2,1:T(4,128)S(1)}, f32[3,1,1,2048]{3,0,2,1:T(4,128)S(1)}, u32[]{:S(2)}, u32[]{:S(2)}) collective-permute-start(f32[3,1,1,2048]{3,0,2,1:T(4,128)S(1)} %get-tuple-element.6), channel_id=1, source_target_pairs={{1,0},{2,1},{3,2},{5,4},{6,5},{7,6},{9,8},{10,9},{11,10},{13,12},{... | collective-permute-start | bytes 73736 | tf_op jit(solution)/shard_map/ppermute | solution.py:20
  17.1 0.7 compare_select_fusion
  17.8 0.7 compare_and_fusion
  18.5 31.9 %all_gather.3 = bf16[2,8,2048]{2,0,1:T(2,128)(2,1)S(1)} all-gather(bf16[2,1,2048]{2,0,1:T(2,128)(2,1)} %param.10), channel_id=1, replica_groups=mesh['angle'=8,'row'=4] {'angle'}, dimensions={1}, use_global_device_ids=true | all-gather | bytes 73728 | tf_op jit(solution)/shard_map/all_gather | solution.py:83
  50.3 0.0 collective-permute-done
  50.3 0.3 fusion.7
  50.6 0.3 fusion.30
  50.9 0.5 broadcast.125
  51.4 0.8 reduce
  52.2 0.6 reshape.272
  52.8 5.5 %all-to-all-start = ((bf16[8,2,1024]{2,1,0:T(2,128)(2,1)}), bf16[8,2,1024]{2,1,0:T(2,128)(2,1)S(1)}, u32[]{:S(2)}, u32[]{:S(2)}) async-start(bf16[8,2,1024]{2,1,0:T(2,128)(2,1)} %reshape.272), calls=%async_computation | async-start | bytes 65536 | tf_op jit(solution)/shard_map/all_to_all | solution.py:85
  58.3 6.7 %all-to-all-done = bf16[8,2,1024]{2,1,0:T(2,128)(2,1)S(1)} async-done(((bf16[8,2,1024]{2,1,0:T(2,128)(2,1)}), bf16[8,2,1024]{2,1,0:T(2,128)(2,1)S(1)}, u32[]{:S(2)}, u32[]{:S(2)}) %all-to-all-start) | async-done | bytes 32800 | tf_op jit(solution)/shard_map/all_to_all | solution.py:85
  65.0 0.6 gather_fusion
  65.6 0.1 bitcast_select_fusion
  65.7 1.3 %rev.3 = bf16[8,1,2048]{2,0,1:T(8,128)(2,1)S(1)} reverse(bf16[8,1,2048]{2,0,1:T(8,128)(2,1)S(1)} %bitcast_select_fusion), dimensions={2} | reverse | bytes 65536 | tf_op jit(solution)/shard_map/rev | solution.py:87
  67.0 8.0 %fusion.22 = f32[8,4096]{1,0:T(8,128)S(1)} fusion(bf16[2048,4096]{1,0:T(8,128)(2,1)} %constant.38, bf16[8,4096]{1,0:T(8,128)(2,1)S(1)} %maximum_bitcast_fusion), kind=kOutput, calls=%fused_computation.49 | convolution fusion | flops 134217728 | bytes 16941056 | tf_op jit(solution)/shard_map/dot_general | solution.py:53
  75.0 14.5 %fusion.4 = bf16[8,1,2048]{2,0,1:T(8,128)(2,1)} fusion(bf16[2048,4096]{1,0:T(8,128)(2,1)} %constant.40, f32[8,4096]{1,0:T(8,128)S(1)} %fusion.22, bf16[2048,4096]{1,0:T(8,128)(2,1)} %constant.38, f32[4096]{0:T(1024)S(1)} %copy-done, bf16[4096]{0:T(1024)(128)(2,1)S(1)} %copy-done.1, bf16[8,4096]{1,0:T(8,128)(2,1)S(1)} %maximum_bitcast_fusion), kind=kOutput, calls=%fused_computation.7 | convolution fusion | flops 268599296 | bytes 33775616 | tf_op jit(solution)/shard_map/dot_general | solution.py:57
  (11 shorter events, 0.1 us)
Async XLA Ops:
  0.0 75.0 %copy-start = (f32[4096]{0:T(1024)S(1)}, f32[4096]{0:T(1024)}, u32[]{:S(2)}) copy-start(f32[4096]{0:T(1024)} %constant.34.clone) | copy-start | bytes 49156
  0.0 75.0 %copy-start.1 = (bf16[4096]{0:T(1024)(128)(2,1)S(1)}, bf16[4096]{0:T(1024)(128)(2,1)}, u32[]{:S(2)}) copy-start(bf16[4096]{0:T(1024)(128)(2,1)} %constant.39) | copy-start | bytes 24580
  13.5 36.9 %collective-permute-start = (f32[3,1,1,2048]{3,0,2,1:T(4,128)S(1)}, f32[3,1,1,2048]{3,0,2,1:T(4,128)S(1)}, u32[]{:S(2)}, u32[]{:S(2)}) collective-permute-start(f32[3,1,1,2048]{3,0,2,1:T(4,128)S(1)} %get-tuple-element.5), channel_id=1, source_target_pairs={{0,1},{1,2},{2,3},{4,5},{5,6},{6,7},{8,9},{9,10},{10,11},{12,13},{... | collective-permute-start | bytes 73736 | tf_op jit(solution)/shard_map/ppermute | solution.py:17
  15.8 34.5 %collective-permute-start.1 = (f32[3,1,1,2048]{3,0,2,1:T(4,128)S(1)}, f32[3,1,1,2048]{3,0,2,1:T(4,128)S(1)}, u32[]{:S(2)}, u32[]{:S(2)}) collective-permute-start(f32[3,1,1,2048]{3,0,2,1:T(4,128)S(1)} %get-tuple-element.6), channel_id=1, source_target_pairs={{1,0},{2,1},{3,2},{5,4},{6,5},{7,6},{9,8},{10,9},{11,10},{13,12},{... | collective-permute-start | bytes 73736 | tf_op jit(solution)/shard_map/ppermute | solution.py:20
  52.8 12.1 %all-to-all-start = ((bf16[8,2,1024]{2,1,0:T(2,128)(2,1)}), bf16[8,2,1024]{2,1,0:T(2,128)(2,1)S(1)}, u32[]{:S(2)}, u32[]{:S(2)}) async-start(bf16[8,2,1024]{2,1,0:T(2,128)(2,1)} %reshape.272), calls=%async_computation | async-start | bytes 65536 | tf_op jit(solution)/shard_map/all_to_all | solution.py:85
where the time goes:
time: 91.2 us; the launch traced here: 89.6 us
  blocking collectives  31.9 us (35%)
  matrix products  22.6 us (25%)
  other arithmetic  14.6 us (16%)
  starting transfers between devices  9.11 us (10%)
  waiting for transfers between devices  6.68 us (7%)
  local copies, waits for them, and re-layouts  4.66 us (5%)
    all_gather x1, blocking collectives, local(): flat_block = lax.all_gather(flat_field, 'angle', axis=1, tiled=True)  31.9 us
    dot_general x1, matrix products, filter_rows(): lax.dot_general(flipped, backward, (((1,), (1,)), ((), ())), preferred_el...  14.5 us
    dot_general x1, matrix products, filter_rows(): jnp.dot(rows[:, :det], forward, preferred_element_type=jnp.float32)  8.04 us
    all_to_all x1, waiting for transfers between devices, local(): lax.all_to_all(dpc, 'angle', split_axis=1, concat_axis=0, tiled=True)  6.68 us
    add x1, other arithmetic, local(): corr_cos = corr_cos + frame * weight_cos[:, step][:, None, None]  5.54 us
    all_to_all x1, starting transfers between devices, local(): lax.all_to_all(dpc, 'angle', split_axis=1, concat_axis=0, tiled=True)  5.46 us
    add x1, other arithmetic, local(): corr_sin = corr_sin + frame * weight_sin[:, step][:, None, None]  5.38 us
    ppermute x1, starting transfers between devices, padded_2(): lax.ppermute(lax.slice_in_dim(block, block.shape[dim] - width, None, axis...  2.36 us
  transfers between devices with their start and end apart: 3, of which 1 were waited for; matrix products, arithmetic and copies ran while one was open for 1% of the time, Pallas kernels for 0%

commit v1 on v0

--- a/solution.py
+++ b/solution.py
@@ -2,6 +2,7 @@
 
 import jax
 import jax.numpy as jnp
+import ml_dtypes
 import numpy as np
 from jax import lax
 from jax.sharding import PartitionSpec as P
@@ -31,33 +32,29 @@
     return (value / smooth_mean.astype(jnp.float32)).astype(jnp.bfloat16)
 
 
-def half_tables(det, padlen):
-    column = np.arange(det, dtype=np.int64)[:, None]
-    freq = np.arange(det, dtype=np.int64)[None, :]
-    theta = (column * freq % padlen).astype(np.float32) * np.float32(two_pi / padlen)
-    cos_half = np.cos(theta).astype(np.float32)
-    sin_half = np.sin(theta).astype(np.float32)
-    forward = np.concatenate([cos_half, sin_half], axis=1)
-    backward = np.concatenate([sin_half, -cos_half], axis=1)
-    parity = np.where(np.arange(det) % 2 == 0, 1.0, -1.0).astype(np.float32)
-    signs = np.concatenate([parity, parity])
-    return (forward, backward, signs)
+def circulant_blocks(padlen, width):
+    count = padlen // width
+    n = np.arange(padlen, dtype=np.float64)
+    odd = np.arange(padlen) % 2 == 1
+    taps = np.where(odd, (2.0 / padlen) / np.tan(np.pi * np.where(odd, n, 1.0) / padlen), 0.0)
+    m = np.arange(count)[:, None, None]
+    p = np.arange(width)[None, :, None]
+    q = np.arange(width)[None, None, :]
+    return taps[(width * m + q - p) % padlen].astype(ml_dtypes.bfloat16)
 
 
 def filter_rows(rows, det):
-    padlen = rows.shape[1]
-    forward_np, backward_np, signs_np = half_tables(det, padlen)
-    forward = jnp.asarray(forward_np).astype(jnp.bfloat16)
-    backward = jnp.asarray(backward_np).astype(jnp.bfloat16)
-    signs = jnp.asarray(signs_np)
-    left_part = jnp.dot(rows[:, :det], forward, preferred_element_type=jnp.float32)
-    right_part = jnp.dot(rows[:, det:], forward, preferred_element_type=jnp.float32)
-    spec = (left_part + right_part * signs[None]).astype(jnp.bfloat16)
-    flipped = spec * signs[None].astype(jnp.bfloat16)
-    total = lax.dot_general(
-        flipped, backward, (((1,), (1,)), ((), ())), preferred_element_type=jnp.float32
-    )
-    return (total * (2.0 / padlen)).astype(jnp.bfloat16)
+    width = 256
+    count, padlen = rows.shape
+    blocks = circulant_blocks(padlen, width)
+    turns, own = padlen // width, det // width
+    table = jnp.asarray(blocks.reshape(padlen, width))
+    cut = rows.reshape(count, turns, width).transpose(1, 0, 2)
+    cut = jnp.concatenate([cut, cut[: own - 1]], axis=0)
+    starts = [(own - m) % turns for m in range(turns)]
+    left = jnp.concatenate([cut[s : s + own] for s in starts], axis=2)
+    total = jnp.dot(left.reshape(own * count, padlen), table, preferred_element_type=jnp.float32)
+    return total.reshape(own, count, width).transpose(1, 0, 2).reshape(count, det).astype(jnp.bfloat16)
 
 
 def local(raw_frames, step_index, partner, flat_field):

time: 91.2 us -> 69.9 us (0.77)
  the two profiles are of different devices: /device:TPU:0 before, /device:TPU:4 now
where the time goes in v1:
time: 69.9 us; the launch traced here: 69.4 us
  blocking collectives  31 us (44%)
  other arithmetic  14.5 us (21%)
  starting transfers between devices  11.1 us (16%)
  waiting for transfers between devices  6.68 us (10%)
  local copies, waits for them, and re-layouts  4.71 us (7%)
  matrix products  1.08 us (2%)
    all_gather x1, blocking collectives, local(): flat_block = lax.all_gather(flat_field, 'angle', axis=1, tiled=True)  31 us
    all_to_all x1, waiting for transfers between devices, local(): lax.all_to_all(dpc, 'angle', split_axis=1, concat_axis=0, tiled=True)  6.68 us
    add x1, other arithmetic, local(): corr_cos = corr_cos + frame * weight_cos[:, step][:, None, None]  5.47 us
    all_to_all x1, starting transfers between devices, local(): lax.all_to_all(dpc, 'angle', split_axis=1, concat_axis=0, tiled=True)  5.45 us
    add x1, other arithmetic, local(): corr_sin = corr_sin + frame * weight_sin[:, step][:, None, None]  5.38 us
    ppermute x1, starting transfers between devices, padded_2(): lax.ppermute(lax.slice_in_dim(block, 0, width, axis=dim), axis, backward)  3.64 us
    ppermute x1, starting transfers between devices, padded_2(): lax.ppermute(lax.slice_in_dim(block, block.shape[dim] - width, None, axis...  2.05 us
  transfers between devices with their start and end apart: 3, of which 1 were waited for; matrix products, arithmetic and copies ran while one was open for 2% of the time, Pallas kernels for 0%

profile of v1, /device:TPU:4, one launch (start us, length us, event | category | flops | bytes accessed | tf_op | source)
XLA Modules:
  0.0 69.4 jit_solution(15449678789903902768)
XLA Ops:
  0.0 0.7 %fusion.27 = (f32[1,8]{1,0:T(1,128)S(1)}, f32[1,8]{1,0:T(1,128)S(1)}) fusion(s32[1,8]{1,0:T(1,128)} %param.6), kind=kLoop, calls=%fused_computation.82 | loop fusion | flops 16 | bytes 96 | tf_op jit(solution)/shard_map/cos | solution.py:63
  0.7 0.9 %fusion.29 = (bf16[1,1,8,2048]{3,2,1,0:T(8,128)(2,1)S(1)}, bf16[1,1,8,2048]{3,2,1,0:T(8,128)(2,1)S(1)}, bf16[1,1,8,2048]{3,2,1,0:T(8,128)(2,1)S(1)}, bf16[1,1,8,...) fusion(bf16[1,8,8,2048]{3,2,1,0:T(8,128)(2,1)} %param.5), kind=kLoop, calls=%fused_computation.84 | loop fusion | bytes 524288 | tf_op jit(solution)/shard_map/slice | solution.py:69
  1.6 0.7 %fusion.30 = (f32[1,1]{1,0:T(1,128)}, f32[1,1]{1,0:T(1,128)}, f32[1,1]{1,0:T(1,128)}, f32[1,1]{1,0:T(1,128)}, f32[1,1]{1,0:T(1,128)}, /*index=5*/f32[1,1]{1,0:T(...) fusion(f32[1,8]{1,0:T(1,128)S(1)} %get-tuple-element.27, ...), kind=kLoop, calls=%fused_computation.85 | loop fusion | bytes 128 | tf_op jit(solution)/shard_map/slice | solution.py:70
  2.3 5.4 %multiply_add_fusion = f32[1,1,8,2048]{3,0,2,1:T(1,128)S(1)} fusion(bf16[1,1,8,2048]{3,2,1,0:T(8,128)(2,1)S(1)} %get-tuple-element.16, bf16[1,1,8,2048]{3,2,1,0:T(8,128)(2,1)S(1)} %get-tuple-element.15, bf16[1,1,8,2048]{3,2,1,0:T(8,128)(2,1)S(1)} %get-tuple-element.14, bf16[1,1,8,2048]{3,2,1,0:T(8,128)(2,1)S(1)} %get-tuple-element.13, ...), kind=kLoop, calls=%fused_computation.48 | loop fusion | flops 376832 | bytes 327712 | tf_op jit(solution)/shard_map/add | solution.py:71
  7.7 5.5 %multiply_add_fusion.1 = (f32[1,1,8,2048]{3,0,2,1:T(1,128)S(1)}, f32[1,1,8,2048]{3,0,2,1:T(1,128)S(1)}) fusion(bf16[1,1,8,2048]{3,2,1,0:T(8,128)(2,1)S(1)} %get-tuple-element.16, bf16[1,1,8,2048]{3,2,1,0:T(8,128)(2,1)S(1)} %get-tuple-element.15, bf16[1,1,8,2048]{3,2,1,0:T(8,128)(2,1)S(1)} %get-tuple-element.14, ...), kind=kLoop, calls=%fused_computation.49 | loop fusion | flops 491520 | bytes 393248 | tf_op jit(solution)/shard_map/add | solution.py:70
  13.2 0.0 copy-start
  13.2 0.2 pad_maximum_fusion.6
  13.4 2.1 %collective-permute-start = (f32[3,1,1,2048]{3,0,2,1:T(4,128)S(1)}, f32[3,1,1,2048]{3,0,2,1:T(4,128)S(1)}, u32[]{:S(2)}, u32[]{:S(2)}) collective-permute-start(f32[3,1,1,2048]{3,0,2,1:T(4,128)S(1)} %get-tuple-element.5), channel_id=1, source_target_pairs={{0,1},{1,2},{2,3},{4,5},{5,6},{6,7},{8,9},{9,10},{10,11},{12,13},{... | collective-permute-start | bytes 73736 | tf_op jit(solution)/shard_map/ppermute | solution.py:18
  15.4 3.6 %collective-permute-start.1 = (f32[3,1,1,2048]{3,0,2,1:T(4,128)S(1)}, f32[3,1,1,2048]{3,0,2,1:T(4,128)S(1)}, u32[]{:S(2)}, u32[]{:S(2)}) collective-permute-start(f32[3,1,1,2048]{3,0,2,1:T(4,128)S(1)} %get-tuple-element.6), channel_id=1, source_target_pairs={{1,0},{2,1},{3,2},{5,4},{6,5},{7,6},{9,8},{10,9},{11,10},{13,12},{... | collective-permute-start | bytes 73736 | tf_op jit(solution)/shard_map/ppermute | solution.py:21
  19.1 0.7 compare_and_fusion
  19.8 0.7 compare_select_fusion
  20.4 31.0 %all_gather.3 = bf16[2,8,2048]{2,0,1:T(2,128)(2,1)S(1)} all-gather(bf16[2,1,2048]{2,0,1:T(2,128)(2,1)} %param.8), channel_id=1, replica_groups=mesh['angle'=8,'row'=4] {'angle'}, dimensions={1}, use_global_device_ids=true | all-gather | bytes 73728 | tf_op jit(solution)/shard_map/all_gather | solution.py:80
  51.5 0.0 collective-permute-done
  51.5 0.3 fusion.2
  51.7 0.3 fusion.32
  52.0 0.5 broadcast.123
  52.5 0.8 %reduce = bf16[8,2048]{1,0:T(8,128)(2,1)S(1)} reduce(bf16[8,1,2048]{2,1,0:T(2,128)(2,1)S(1)} %fusion.32, bf16[]{:T(256)} %broadcast.123), dimensions={1}, to_apply=%fusion.32.reduce_sub_computation | reduce | bytes 65538
  53.3 0.6 reshape.279
  54.0 5.5 %all-to-all-start = ((bf16[8,2,1024]{2,1,0:T(2,128)(2,1)}), bf16[8,2,1024]{2,1,0:T(2,128)(2,1)S(1)}, u32[]{:S(2)}, u32[]{:S(2)}) async-start(bf16[8,2,1024]{2,1,0:T(2,128)(2,1)} %reshape.279), calls=%async_computation | async-start | bytes 65536 | tf_op jit(solution)/shard_map/all_to_all | solution.py:82
  59.4 6.7 %all-to-all-done = bf16[8,2,1024]{2,1,0:T(2,128)(2,1)S(1)} async-done(((bf16[8,2,1024]{2,1,0:T(2,128)(2,1)}), bf16[8,2,1024]{2,1,0:T(2,128)(2,1)S(1)}, u32[]{:S(2)}, u32[]{:S(2)}) %all-to-all-start) | async-done | bytes 32800 | tf_op jit(solution)/shard_map/all_to_all | solution.py:82
  66.2 0.6 gather_fusion
  66.8 0.1 bitcast_select_fusion
  66.8 1.3 %rev.3 = bf16[8,1,2048]{2,0,1:T(8,128)(2,1)S(1)} reverse(bf16[8,1,2048]{2,0,1:T(8,128)(2,1)S(1)} %bitcast_select_fusion), dimensions={2} | reverse | bytes 65536 | tf_op jit(solution)/shard_map/rev | solution.py:84
  68.3 1.1 %convolution_convert_fusion = bf16[8,8,256]{2,1,0:T(8,128)(2,1)} fusion(bf16[8,8,4096]{2,1,0:T(8,128)(2,1)S(1)} %fusion.25, bf16[4096,256,1]{1,0,2:T(8,128)(2,1)S(1)} %copy-done), kind=kOutput, calls=%fused_computation.1 | convolution fusion | flops 134234112 | bytes 2654208 | tf_op jit(solution)/shard_map/dot_general | solution.py:56
  (25 shorter events, 0.2 us)
Async XLA Ops:
  13.2 55.2 %copy-start = (bf16[4096,256,1]{1,0,2:T(8,128)(2,1)S(1)}, bf16[4096,256,1]{1,0,2:T(8,128)(2,1)}, u32[]{:S(2)}) copy-start(bf16[4096,256,1]{1,0,2:T(8,128)(2,1)} %constant.30) | copy-start | bytes 6291460
  13.4 38.1 %collective-permute-start = (f32[3,1,1,2048]{3,0,2,1:T(4,128)S(1)}, f32[3,1,1,2048]{3,0,2,1:T(4,128)S(1)}, u32[]{:S(2)}, u32[]{:S(2)}) collective-permute-start(f32[3,1,1,2048]{3,0,2,1:T(4,128)S(1)} %get-tuple-element.5), channel_id=1, source_target_pairs={{0,1},{1,2},{2,3},{4,5},{5,6},{6,7},{8,9},{9,10},{10,11},{12,13},{... | collective-permute-start | bytes 73736 | tf_op jit(solution)/shard_map/ppermute | solution.py:18
  15.4 36.0 %collective-permute-start.1 = (f32[3,1,1,2048]{3,0,2,1:T(4,128)S(1)}, f32[3,1,1,2048]{3,0,2,1:T(4,128)S(1)}, u32[]{:S(2)}, u32[]{:S(2)}) collective-permute-start(f32[3,1,1,2048]{3,0,2,1:T(4,128)S(1)} %get-tuple-element.6), channel_id=1, source_target_pairs={{1,0},{2,1},{3,2},{5,4},{6,5},{7,6},{9,8},{10,9},{11,10},{13,12},{... | collective-permute-start | bytes 73736 | tf_op jit(solution)/shard_map/ppermute | solution.py:21
  54.0 12.1 %all-to-all-start = ((bf16[8,2,1024]{2,1,0:T(2,128)(2,1)}), bf16[8,2,1024]{2,1,0:T(2,128)(2,1)S(1)}, u32[]{:S(2)}, u32[]{:S(2)}) async-start(bf16[8,2,1024]{2,1,0:T(2,128)(2,1)} %reshape.279), calls=%async_computation | async-start | bytes 65536 | tf_op jit(solution)/shard_map/all_to_all | solution.py:82

commit v2 on v1

v2 whole, which is shorter than its diff:
```python
import math

import jax
import jax.numpy as jnp
import ml_dtypes
import numpy as np
from jax import lax
from jax.experimental import pallas as pl
from jax.experimental.pallas import tpu as pltpu
from jax.sharding import PartitionSpec as P

WIDTH = 256
LANES = 128


def circulant_blocks(padlen):
    count = padlen // WIDTH
    n = np.arange(padlen, dtype=np.float64)
    odd = np.arange(padlen) % 2 == 1
    taps = np.where(odd, (2.0 / padlen) / np.tan(np.pi * np.where(odd, n, 1.0) / padlen), 0.0)
    m = np.arange(count)[:, None, None]
    p = np.arange(WIDTH)[None, :, None]
    q = np.arange(WIDTH)[None, None, :]
    blocks = taps[(WIDTH * m + q - p) % padlen]
    reverse = -np.eye(WIDTH)[::-1][None]
    return np.concatenate([blocks, reverse], axis=0).astype(ml_dtypes.bfloat16)


def loop(start, stop, body):
    if stop - start <= 8:
        for i in range(start, stop):
            body(i)
    else:
        lax.fori_loop(start, stop, lambda i, _: body(i), None)


def kernel(
    angles, blocks_row, raw_hbm, step_ref, partner_ref, flat_ref, table_hbm, out_ref,
    raw, table, corr, halo, smooth, recv, stage, mirror, ring,
    local_sem, halo_send, halo_recv, send_sem, recv_sem,
):
    steps, rows, det = raw.shape
    chunks = det // LANES
    own = det // WIDTH
    me = lax.axis_index("angle")
    row = lax.axis_index("row")
    after = lax.rem(row + 1, blocks_row)
    before = lax.rem(row + blocks_row - 1, blocks_row)

    barrier = pltpu.get_barrier_semaphore()

    def greet(k):
        pl.semaphore_signal(barrier, inc=1, device_id={"angle": lax.rem(me + k, angles)})

    raw_copy = pltpu.make_async_copy(raw_hbm.at[0], raw, local_sem.at[0])
    raw_copy.start()
    pl.semaphore_signal(barrier, inc=1, device_id={"row": after})
    pl.semaphore_signal(barrier, inc=1, device_id={"row": before})
    loop(1, angles, greet)
    table_copy = pltpu.make_async_copy(table_hbm, table, local_sem.at[1])
    table_copy.start()

    def weight(k, values):
        index = step_ref[0, k]
        value = jnp.float32(values[0])
        for i in range(1, steps):
            value = jnp.where(index == i, jnp.float32(values[i]), value)
        return value

    grid = 2.0 * math.pi * np.arange(steps) / steps
    cosines = [weight(k, np.cos(grid).astype(np.float32)) for k in range(steps)]
    sines = [weight(k, np.sin(grid).astype(np.float32)) for k in range(steps)]
    raw_copy.wait()

    def correlate(g):
        at = g * 8 if isinstance(g, int) else pl.multiple_of(g * 8, 8)
        for c in range(chunks):
            sums = [None, None, None]
            for k in range(steps):
                frame = raw[k, pl.ds(at, 8), c * LANES : (c + 1) * LANES].astype(jnp.float32)
                terms = [frame * cosines[k], frame * sines[k], frame]
                sums = terms if k == 0 else [s + t for s, t in zip(sums, terms)]
            for q in range(3):
                corr[q, pl.ds(at * chunks + c, 8, stride=chunks), :] = sums[q]

    loop(0, rows // 8, correlate)

    pl.semaphore_wait(barrier, angles + 1)

    def halo_copy(side, first, target):
        return pltpu.make_async_remote_copy(
            src_ref=corr.at[:, pl.ds(first * chunks, chunks), :],
            dst_ref=halo.at[side],
            send_sem=halo_send.at[side],
            recv_sem=halo_recv.at[side],
            device_id={"row": target},
        )

    low = halo_copy(0, rows - 1, after)
    high = halo_copy(1, 0, before)
    low.start()
    high.start()

    def line(q, i):
        at = i * chunks if isinstance(i, int) else pl.multiple_of(i * chunks, chunks)
        return corr[q, pl.ds(at, chunks), :]

    def interior(i):
        for q in range(3):
            value = 0.25 * line(q, i - 1) + 0.5 * line(q, i) + 0.25 * line(q, i + 1)
            smooth[i, q] = value.astype(jnp.bfloat16)

    loop(1, rows - 1, interior)

    def row_copy(target):
        return pltpu.make_async_remote_copy(
            src_ref=smooth.at[target],
            dst_ref=recv.at[me],
            send_sem=send_sem.at[target],
            recv_sem=recv_sem.at[me],
            device_id={"angle": target},
        )

    def send_interior(k):
        target = lax.rem(me + k, angles)

        @pl.when((target != 0) & (target != angles - 1))
        def _():
            row_copy(target).start()

    loop(1, angles, send_interior)

    low.wait_recv()
    high.wait_recv()
    for q in range(3):
        edge = jnp.where(row == 0, 0.0, halo[0, q])
        value = 0.25 * edge + 0.5 * line(q, 0) + 0.25 * line(q, 1)
        smooth[0, q] = value.astype(jnp.bfloat16)
    for q in range(3):
        edge = jnp.where(row == blocks_row - 1, 0.0, halo[1, q])
        value = 0.25 * line(q, rows - 2) + 0.5 * line(q, rows - 1) + 0.25 * edge
        smooth[rows - 1, q] = value.astype(jnp.bfloat16)
    for target in (0, angles - 1):
        @pl.when(target != me)
        def _():
            row_copy(target).start()

    recv[me] = smooth[me]
    table_copy.wait()

    def arrived(k):
        source = lax.rem(me + angles - k, angles)
        pltpu.make_async_remote_copy(
            src_ref=smooth.at[source],
            dst_ref=recv.at[source],
            send_sem=send_sem.at[source],
            recv_sem=recv_sem.at[source],
            device_id={"angle": source},
        ).wait_recv()

    loop(1, angles, arrived)

    def spread(a):
        other = partner_ref[a]
        for q in range(3):
            at = a * chunks if isinstance(a, int) else pl.multiple_of(a * chunks, chunks)
            stage[q, pl.ds(at, chunks), :] = recv[a, q].astype(jnp.float32)
            stage[q, pl.ds(at + angles * chunks, chunks), :] = recv[other, q].astype(jnp.float32)

    loop(0, angles, spread)

    flat_cos = flat_ref[0].astype(jnp.float32)
    flat_sin = flat_ref[1].astype(jnp.float32)
    for c in range(chunks):
        lanes = slice(c * LANES, (c + 1) * LANES)
        part = [stage[q, pl.ds(c, 2 * angles, stride=chunks), :] for q in range(3)]
        value = steps * (part[1] * flat_cos[:, lanes] - part[0] * flat_sin[:, lanes]) / part[2]
        dpc = value.astype(jnp.bfloat16).astype(jnp.float32)
        block = c // (WIDTH // LANES)
        at = (c % (WIDTH // LANES)) * LANES
        ring[(own + block) * angles : (own + block + 1) * angles, at : at + LANES] = dpc[:angles]
        back = own - 1 - block
        mirror[back * angles : (back + 1) * angles, at : at + LANES] = dpc[angles:]

    turns = 2 * own
    flipped = jnp.dot(
        mirror[...].astype(jnp.bfloat16), table[turns], preferred_element_type=jnp.float32
    )
    ring[: own * angles] = flipped
    ring[turns * angles : (turns + own) * angles] = flipped

    total = jnp.zeros((own * angles, WIDTH), jnp.float32)
    for m in range(turns):
        first = (own - m) % turns
        window = ring[first * angles : (first + own) * angles].astype(jnp.bfloat16)
        total = total + jnp.dot(window, table[m], preferred_element_type=jnp.float32)
    for block in range(own):
        out_ref[:, block * WIDTH : (block + 1) * WIDTH] = total[
            block * angles : (block + 1) * angles
        ].astype(jnp.bfloat16)

    def sent(k):
        row_copy(lax.rem(me + k, angles)).wait_send()

    loop(1, angles, sent)
    low.wait_send()
    high.wait_send()


def local(raw_frames, step_index, partner, flat_field):
    _, steps, rows, det = raw_frames.shape
    angles = lax.axis_size("angle")
    blocks_row = lax.axis_size("row")
    chunks = det // LANES
    own = det // WIDTH
    assert rows == angles and rows % 8 == 0 and raw_frames.shape[0] == 1
    table = jnp.asarray(circulant_blocks(2 * det))
    body = lambda *refs: kernel(angles, blocks_row, *refs)
    result = pl.pallas_call(
        body,
        out_shape=jax.ShapeDtypeStruct((angles, det), jnp.bfloat16),
        in_specs=[
            pl.BlockSpec(memory_space=pl.ANY),
            pl.BlockSpec(memory_space=pltpu.SMEM),
            pl.BlockSpec(memory_space=pltpu.SMEM),
            pl.BlockSpec(memory_space=pltpu.VMEM),
            pl.BlockSpec(memory_space=pl.ANY),
        ],
        out_specs=pl.BlockSpec(memory_space=pltpu.VMEM),
        scratch_shapes=[
            pltpu.VMEM((steps, rows, det), jnp.bfloat16),
            pltpu.VMEM(table.shape, jnp.bfloat16),
            pltpu.VMEM((3, rows * chunks, LANES), jnp.float32),
            pltpu.VMEM((2, 3, chunks, LANES), jnp.float32),
            pltpu.VMEM((rows, 3, chunks, LANES), jnp.bfloat16),
            pltpu.VMEM((angles, 3, chunks, LANES), jnp.bfloat16),
            pltpu.VMEM((3, 2 * angles * chunks, LANES), jnp.float32),
            pltpu.VMEM((own * angles, WIDTH), jnp.float32),
            pltpu.VMEM((3 * own * angles, WIDTH), jnp.float32),
            pltpu.SemaphoreType.DMA((2,)),
            pltpu.SemaphoreType.DMA((2,)),
            pltpu.SemaphoreType.DMA((2,)),
            pltpu.SemaphoreType.DMA((angles,)),
            pltpu.SemaphoreType.DMA((angles,)),
        ],
        compiler_params=pltpu.CompilerParams(
            collective_id=0, has_side_effects=True, vmem_limit_bytes=48 * 1024 * 1024
        ),
    )(raw_frames, step_index, partner, flat_field, table)
    return result[:, None, :]


def solution(mesh):
    in_specs = (
        P("angle", None, "row", None),
        P("angle", None),
        P(),
        P(None, ("row", "angle"), None),
    )
    out_specs = P(None, ("row", "angle"), None)
    return jax.shard_map(local, mesh=mesh, in_specs=in_specs, out_specs=out_specs, check_vma=False)
```

time: 69.9 us -> 17.9 us (0.26)
  the two profiles are of different devices: /device:TPU:4 before, /device:TPU:0 now
where the time goes in v2:
time: 17.9 us; the launch traced here: 17.6 us
  Pallas kernels  12.4 us (69%)
  local copies, waits for them, and re-layouts  5.21 us (29%)
    pallas_call x1, Pallas kernels, local(): pl.pallas_call(body, out_shape=jax.ShapeDtypeStruct((angles, det), jnp.bf...  12.4 us
    unnamed x10, local copies, waits for them, and re-layouts  5.21 us

profile of v2, /device:TPU:0, one launch (start us, length us, event | category | flops | bytes accessed | tf_op | source)
XLA Modules:
  0.0 17.6 jit_solution(12381577791409307086)
XLA Ops:
  0.0 0.7 %copy.6.refs_3_ = bf16[2,1,2048]{2,1,0:T(2,128)(2,1)S(1)} copy(bf16[2,1,2048]{2,0,1:T(2,128)(2,1)} %param.8) | data formatting | bytes 16384 | tf_op args[3]
  0.7 0.0 copy-start
  0.7 1.6 %copy-done = bf16[17,256,256]{2,1,0:T(8,128)(2,1)S(1)} copy-done((bf16[17,256,256]{2,1,0:T(8,128)(2,1)S(1)}, bf16[17,256,256]{2,1,0:T(8,128)(2,1)}, u32[]{:S(2)}) %copy-start) | copy-done | bytes 2228248
  2.3 0.0 copy-start.1
  2.3 0.9 %copy-done.1 = bf16[1,8,8,2048]{3,2,1,0:T(8,128)(2,1)S(1)} copy-done((bf16[1,8,8,2048]{3,2,1,0:T(8,128)(2,1)S(1)}, bf16[1,8,8,2048]{3,2,1,0:T(8,128)(2,1)}, u32[]{:S(2)}) %copy-start.1) | copy-done | bytes 262168
  3.3 0.0 copy-start.2
  3.3 0.7 %copy-done.2 = s32[1,8]{1,0:T(1,128)S(1)} copy-done((s32[1,8]{1,0:T(1,128)S(1)}, s32[1,8]{1,0:T(1,128)}, u32[]{:S(2)}) %copy-start.2) | copy-done | bytes 56
  4.0 0.0 copy-start.3
  4.0 0.7 %copy-done.3 = s32[8]{0:T(128)S(1)} copy-done((s32[8]{0:T(128)S(1)}, s32[8]{0:T(128)}, u32[]{:S(2)}) %copy-start.3) | copy-done | bytes 56
  4.6 12.4 %shard_map.55 = bf16[8,2048]{1,0:T(8,128)(2,1)S(1)} custom-call(bf16[1,8,8,2048]{3,2,1,0:T(8,128)(2,1)S(1)} %copy-done.1, s32[1,8]{1,0:T(1,128)S(1)} %copy-done.2, s32[8]{0:T(128)S(1)} %copy-done.3, bf16[2,1,2048]{2,1,0:T(2,128)(2,1)S(1)} %copy.6.refs_3_, bf16[17,256,256]{2,1,0:T(8,128)(2,1)S(1)} %copy-done), custom_call_target="tpu_custom_call" | custom-call | tf_op jit(solution)/shard_map/pallas_call | solution.py:219
  17.0 0.6 %copy.8 = bf16[8,1,2048]{2,0,1:T(8,128)(2,1)} copy(bf16[8,1,2048]{2,0,1:T(8,128)(2,1)S(1)} %bitcast.1) | data formatting | bytes 65536
Async XLA Ops:
  0.7 1.6 %copy-start = (bf16[17,256,256]{2,1,0:T(8,128)(2,1)S(1)}, bf16[17,256,256]{2,1,0:T(8,128)(2,1)}, u32[]{:S(2)}) copy-start(bf16[17,256,256]{2,1,0:T(8,128)(2,1)} %constant.2.clone.refs_4_) | copy-start | bytes 6684676
  2.3 0.9 %copy-start.1 = (bf16[1,8,8,2048]{3,2,1,0:T(8,128)(2,1)S(1)}, bf16[1,8,8,2048]{3,2,1,0:T(8,128)(2,1)}, u32[]{:S(2)}) copy-start(bf16[1,8,8,2048]{3,2,1,0:T(8,128)(2,1)} %refs_0_.1) | copy-start | bytes 786436
  3.3 0.7 %copy-start.2 = (s32[1,8]{1,0:T(1,128)S(1)}, s32[1,8]{1,0:T(1,128)}, u32[]{:S(2)}) copy-start(s32[1,8]{1,0:T(1,128)} %refs_1_.1) | copy-start | bytes 100
  4.0 0.7 %copy-start.3 = (s32[8]{0:T(128)S(1)}, s32[8]{0:T(128)}, u32[]{:S(2)}) copy-start(s32[8]{0:T(128)} %refs_2_.1) | copy-start | bytes 100

commit v3 on v2

--- a/solution.py
+++ b/solution.py
@@ -35,8 +35,8 @@
 
 
 def kernel(
-    angles, blocks_row, raw_hbm, step_ref, partner_ref, flat_ref, table_hbm, out_ref,
-    raw, table, corr, halo, smooth, recv, stage, mirror, ring,
+    angles, blocks_row, raw_hbm, step_hbm, partner_hbm, flat_hbm, table_hbm, out_ref,
+    raw, table, step_ref, partner_ref, flat_ref, corr, halo, smooth, recv, stage, mirror, ring,
     local_sem, halo_send, halo_recv, send_sem, recv_sem,
 ):
     steps, rows, det = raw.shape
@@ -54,11 +54,18 @@
 
     raw_copy = pltpu.make_async_copy(raw_hbm.at[0], raw, local_sem.at[0])
     raw_copy.start()
+    step_copy = pltpu.make_async_copy(step_hbm, step_ref, local_sem.at[2])
+    step_copy.start()
     pl.semaphore_signal(barrier, inc=1, device_id={"row": after})
     pl.semaphore_signal(barrier, inc=1, device_id={"row": before})
     loop(1, angles, greet)
     table_copy = pltpu.make_async_copy(table_hbm, table, local_sem.at[1])
     table_copy.start()
+    partner_copy = pltpu.make_async_copy(partner_hbm, partner_ref, local_sem.at[3])
+    partner_copy.start()
+    flat_copy = pltpu.make_async_copy(flat_hbm, flat_ref, local_sem.at[4])
+    flat_copy.start()
+    step_copy.wait()
 
     def weight(k, values):
         index = step_ref[0, k]
@@ -147,6 +154,8 @@
 
     recv[me] = smooth[me]
     table_copy.wait()
+    partner_copy.wait()
+    flat_copy.wait()
 
     def arrived(k):
         source = lax.rem(me + angles - k, angles)
@@ -169,8 +178,8 @@
 
     loop(0, angles, spread)
 
-    flat_cos = flat_ref[0].astype(jnp.float32)
-    flat_sin = flat_ref[1].astype(jnp.float32)
+    flat = flat_ref[...].astype(jnp.float32)
+    flat_cos, flat_sin = flat[0:1], flat[1:2]
     for c in range(chunks):
         lanes = slice(c * LANES, (c + 1) * LANES)
         part = [stage[q, pl.ds(c, 2 * angles, stride=chunks), :] for q in range(3)]
@@ -219,17 +228,14 @@
     result = pl.pallas_call(
         body,
         out_shape=jax.ShapeDtypeStruct((angles, det), jnp.bfloat16),
-        in_specs=[
-            pl.BlockSpec(memory_space=pl.ANY),
-            pl.BlockSpec(memory_space=pltpu.SMEM),
-            pl.BlockSpec(memory_space=pltpu.SMEM),
-            pl.BlockSpec(memory_space=pltpu.VMEM),
-            pl.BlockSpec(memory_space=pl.ANY),
-        ],
+        in_specs=[pl.BlockSpec(memory_space=pltpu.HBM)] * 5,
         out_specs=pl.BlockSpec(memory_space=pltpu.VMEM),
         scratch_shapes=[
             pltpu.VMEM((steps, rows, det), jnp.bfloat16),
             pltpu.VMEM(table.shape, jnp.bfloat16),
+            pltpu.SMEM((1, steps), jnp.int32),
+            pltpu.SMEM((angles,), jnp.int32),
+            pltpu.VMEM((2, det), jnp.bfloat16),
             pltpu.VMEM((3, rows * chunks, LANES), jnp.float32),
             pltpu.VMEM((2, 3, chunks, LANES), jnp.float32),
             pltpu.VMEM((rows, 3, chunks, LANES), jnp.bfloat16),
@@ -237,7 +243,7 @@
             pltpu.VMEM((3, 2 * angles * chunks, LANES), jnp.float32),
             pltpu.VMEM((own * angles, WIDTH), jnp.float32),
             pltpu.VMEM((3 * own * angles, WIDTH), jnp.float32),
-            pltpu.SemaphoreType.DMA((2,)),
+            pltpu.SemaphoreType.DMA((5,)),
             pltpu.SemaphoreType.DMA((2,)),
             pltpu.SemaphoreType.DMA((2,)),
             pltpu.SemaphoreType.DMA((angles,)),
@@ -246,7 +252,7 @@
         compiler_params=pltpu.CompilerParams(
             collective_id=0, has_side_effects=True, vmem_limit_bytes=48 * 1024 * 1024
         ),
-    )(raw_frames, step_index, partner, flat_field, table)
+    )(raw_frames, step_index, partner, flat_field[:, 0, :], table)
     return result[:, None, :]
 
 

time: 17.9 us -> 17.4 us (0.972)
  Pallas kernels: 12.4 us -> 12 us
    pallas_call x1, Pallas kernels: 12.4 us -> 12 us  [local(): pl.pallas_call(body, out_shape=jax.ShapeDtypeStruct((angles, det), jnp.bf...]
    unnamed x10 -> x11, local copies, waits for them, and re-layouts: 5.21 us -> 5.2 us
where the time goes in v3:
time: 17.4 us; the launch traced here: 17.2 us
  Pallas kernels  12 us (69%)
  local copies, waits for them, and re-layouts  5.2 us (30%)
    pallas_call x1, Pallas kernels, local(): pl.pallas_call(body, out_shape=jax.ShapeDtypeStruct((angles, det), jnp.bf...  12 us
    unnamed x11, local copies, waits for them, and re-layouts  5.2 us

profile of v3, /device:TPU:0, one launch (start us, length us, event | category | flops | bytes accessed | tf_op | source)
XLA Modules:
  0.0 17.2 jit_solution(7207107143359019400)
XLA Ops:
  0.0 0.0 copy-start
  0.0 1.6 %copy-done = bf16[17,256,256]{2,1,0:T(8,128)(2,1)S(1)} copy-done((bf16[17,256,256]{2,1,0:T(8,128)(2,1)S(1)}, bf16[17,256,256]{2,1,0:T(8,128)(2,1)}, u32[]{:S(2)}) %copy-start) | copy-done | bytes 2228248
  1.6 0.0 copy-start.1
  1.6 0.9 %copy-done.1 = bf16[1,8,8,2048]{3,2,1,0:T(8,128)(2,1)S(1)} copy-done((bf16[1,8,8,2048]{3,2,1,0:T(8,128)(2,1)S(1)}, bf16[1,8,8,2048]{3,2,1,0:T(8,128)(2,1)}, u32[]{:S(2)}) %copy-start.1) | copy-done | bytes 262168
  2.6 0.0 copy-start.2
  2.6 0.7 %copy-done.2 = bf16[2,1,2048]{2,0,1:T(2,128)(2,1)S(1)} copy-done((bf16[2,1,2048]{2,0,1:T(2,128)(2,1)S(1)}, bf16[2,1,2048]{2,0,1:T(2,128)(2,1)}, u32[]{:S(2)}) %copy-start.2) | copy-done | bytes 8216
  3.3 0.0 copy-start.3
  3.3 0.7 %copy-done.3 = s32[1,8]{1,0:T(1,128)S(1)} copy-done((s32[1,8]{1,0:T(1,128)S(1)}, s32[1,8]{1,0:T(1,128)}, u32[]{:S(2)}) %copy-start.3) | copy-done | bytes 56
  3.9 0.0 copy-start.4
  3.9 0.7 %copy-done.4 = s32[8]{0:T(128)S(1)} copy-done((s32[8]{0:T(128)S(1)}, s32[8]{0:T(128)}, u32[]{:S(2)}) %copy-start.4) | copy-done | bytes 56
  4.6 12.0 %shard_map.55 = bf16[8,2048]{1,0:T(8,128)(2,1)S(1)} custom-call(bf16[1,8,8,2048]{3,2,1,0:T(8,128)(2,1)S(1)} %copy-done.1, s32[1,8]{1,0:T(1,128)S(1)} %copy-done.3, s32[8]{0:T(128)S(1)} %copy-done.4, bf16[2,2048]{1,0:T(2,128)(2,1)S(1)} %bitcast.3, bf16[17,256,256]{2,1,0:T(8,128)(2,1)S(1)} %copy-done), custom_call_target="tpu_custom_call" | custom-call | tf_op jit(solution)/shard_map/pallas_call | solution.py:228
  16.6 0.6 %copy.7 = bf16[8,1,2048]{2,0,1:T(8,128)(2,1)} copy(bf16[8,1,2048]{2,0,1:T(8,128)(2,1)S(1)} %bitcast.2) | data formatting | bytes 65536
Async XLA Ops:
  0.0 1.6 %copy-start = (bf16[17,256,256]{2,1,0:T(8,128)(2,1)S(1)}, bf16[17,256,256]{2,1,0:T(8,128)(2,1)}, u32[]{:S(2)}) copy-start(bf16[17,256,256]{2,1,0:T(8,128)(2,1)} %constant.2.clone.refs_4_) | copy-start | bytes 6684676
  1.6 0.9 %copy-start.1 = (bf16[1,8,8,2048]{3,2,1,0:T(8,128)(2,1)S(1)}, bf16[1,8,8,2048]{3,2,1,0:T(8,128)(2,1)}, u32[]{:S(2)}) copy-start(bf16[1,8,8,2048]{3,2,1,0:T(8,128)(2,1)} %refs_0_.1) | copy-start | bytes 786436
  2.6 0.7 %copy-start.2 = (bf16[2,1,2048]{2,0,1:T(2,128)(2,1)S(1)}, bf16[2,1,2048]{2,0,1:T(2,128)(2,1)}, u32[]{:S(2)}) copy-start(bf16[2,1,2048]{2,0,1:T(2,128)(2,1)} %param.8) | copy-start | bytes 24580
  3.3 0.7 %copy-start.3 = (s32[1,8]{1,0:T(1,128)S(1)}, s32[1,8]{1,0:T(1,128)}, u32[]{:S(2)}) copy-start(s32[1,8]{1,0:T(1,128)} %refs_1_.1) | copy-start | bytes 100
  3.9 0.7 %copy-start.4 = (s32[8]{0:T(128)S(1)}, s32[8]{0:T(128)}, u32[]{:S(2)}) copy-start(s32[8]{0:T(128)} %refs_2_.1) | copy-start | bytes 100

commit v4 on v3

--- a/solution.py
+++ b/solution.py
@@ -252,7 +252,7 @@
         compiler_params=pltpu.CompilerParams(
             collective_id=0, has_side_effects=True, vmem_limit_bytes=48 * 1024 * 1024
         ),
-    )(raw_frames, step_index, partner, flat_field[:, 0, :], table)
+    )(*[pltpu.with_memory_space_constraint(x, pltpu.HBM) for x in (raw_frames, step_index, partner, flat_field[:, 0, :], table)])
     return result[:, None, :]
 
 

time: 17.4 us -> 13 us (0.75)
  local copies, waits for them, and re-layouts: 5.2 us -> 0.62 us
  Pallas kernels: 12 us -> 12.3 us
    unnamed x11 -> x1, local copies, waits for them, and re-layouts: 5.2 us -> 0.62 us
    pallas_call x1, Pallas kernels: 12 us -> 12.3 us  [local(): pl.pallas_call(body, out_shape=jax.ShapeDtypeStruct((angles, det), jnp.bf...]
where the time goes in v4:
time: 13 us; the launch traced here: 12.9 us
  Pallas kernels  12.3 us (95%)
  local copies, waits for them, and re-layouts  0.62 us (5%)
    pallas_call x1, Pallas kernels, local(): pl.pallas_call(body, out_shape=jax.ShapeDtypeStruct((angles, det), jnp.bf...  12.3 us
    unnamed x1, local copies, waits for them, and re-layouts  0.62 us

profile of v4, /device:TPU:0, one launch (start us, length us, event | category | flops | bytes accessed | tf_op | source)
XLA Modules:
  0.0 12.9 jit_solution(17160008981244807923)
XLA Ops:
  0.0 12.3 %shard_map.55 = bf16[8,2048]{1,0:T(8,128)(2,1)S(1)} custom-call(bf16[1,8,8,2048]{3,2,1,0:T(8,128)(2,1)} %refs_0_.1, s32[1,8]{1,0:T(1,128)} %refs_1_.1, s32[8]{0:T(128)} %refs_2_.1, bf16[2,2048]{1,0:T(2,128)(2,1)} %bitcast.3, bf16[17,256,256]{2,1,0:T(8,128)(2,1)} %constant.2.clone.refs_4_), custom_call_target="tpu_custom_call" | custom-call | tf_op jit(solution)/shard_map/pallas_call | solution.py:228
  12.3 0.6 %copy.7 = bf16[8,1,2048]{2,0,1:T(8,128)(2,1)} copy(bf16[8,1,2048]{2,0,1:T(8,128)(2,1)S(1)} %bitcast.2) | data formatting | bytes 65536

commit v5 on v4

--- a/solution.py
+++ b/solution.py
@@ -56,9 +56,27 @@
     raw_copy.start()
     step_copy = pltpu.make_async_copy(step_hbm, step_ref, local_sem.at[2])
     step_copy.start()
-    pl.semaphore_signal(barrier, inc=1, device_id={"row": after})
-    pl.semaphore_signal(barrier, inc=1, device_id={"row": before})
+    has_before = row > 0
+    has_after = row < blocks_row - 1
+
     loop(1, angles, greet)
+
+    @pl.when(has_after)
+    def _():
+        pl.semaphore_signal(barrier, inc=1, device_id={"row": after})
+
+    @pl.when(has_before)
+    def _():
+        pl.semaphore_signal(barrier, inc=1, device_id={"row": before})
+
+    @pl.when(row == 0)
+    def _():
+        halo[0] = jnp.zeros_like(halo[0])
+
+    @pl.when(row == blocks_row - 1)
+    def _():
+        halo[1] = jnp.zeros_like(halo[1])
+
     table_copy = pltpu.make_async_copy(table_hbm, table, local_sem.at[1])
     table_copy.start()
     partner_copy = pltpu.make_async_copy(partner_hbm, partner_ref, local_sem.at[3])
@@ -92,7 +110,9 @@
 
     loop(0, rows // 8, correlate)
 
-    pl.semaphore_wait(barrier, angles + 1)
+    pl.semaphore_wait(
+        barrier, angles - 1 + has_before.astype(jnp.int32) + has_after.astype(jnp.int32)
+    )
 
     def halo_copy(side, first, target):
         return pltpu.make_async_remote_copy(
@@ -105,8 +125,14 @@
 
     low = halo_copy(0, rows - 1, after)
     high = halo_copy(1, 0, before)
-    low.start()
-    high.start()
+
+    @pl.when(has_after)
+    def _():
+        low.start()
+
+    @pl.when(has_before)
+    def _():
+        high.start()
 
     def line(q, i):
         at = i * chunks if isinstance(i, int) else pl.multiple_of(i * chunks, chunks)
@@ -128,29 +154,29 @@
             device_id={"angle": target},
         )
 
-    def send_interior(k):
-        target = lax.rem(me + k, angles)
-
-        @pl.when((target != 0) & (target != angles - 1))
-        def _():
-            row_copy(target).start()
-
-    loop(1, angles, send_interior)
-
-    low.wait_recv()
-    high.wait_recv()
-    for q in range(3):
-        edge = jnp.where(row == 0, 0.0, halo[0, q])
-        value = 0.25 * edge + 0.5 * line(q, 0) + 0.25 * line(q, 1)
-        smooth[0, q] = value.astype(jnp.bfloat16)
-    for q in range(3):
-        edge = jnp.where(row == blocks_row - 1, 0.0, halo[1, q])
-        value = 0.25 * line(q, rows - 2) + 0.5 * line(q, rows - 1) + 0.25 * edge
-        smooth[rows - 1, q] = value.astype(jnp.bfloat16)
-    for target in (0, angles - 1):
+    def send(target):
         @pl.when(target != me)
         def _():
             row_copy(target).start()
+
+    @pl.when(has_before)
+    def _():
+        low.wait_recv()
+
+    for q in range(3):
+        value = 0.25 * halo[0, q] + 0.5 * line(q, 0) + 0.25 * line(q, 1)
+        smooth[0, q] = value.astype(jnp.bfloat16)
+    send(0)
+    loop(1, angles - 1, send)
+
+    @pl.when(has_after)
+    def _():
+        high.wait_recv()
+
+    for q in range(3):
+        value = 0.25 * line(q, rows - 2) + 0.5 * line(q, rows - 1) + 0.25 * halo[1, q]
+        smooth[rows - 1, q] = value.astype(jnp.bfloat16)
+    send(angles - 1)
 
     recv[me] = smooth[me]
     table_copy.wait()
@@ -212,8 +238,14 @@
         row_copy(lax.rem(me + k, angles)).wait_send()
 
     loop(1, angles, sent)
-    low.wait_send()
-    high.wait_send()
+
+    @pl.when(has_after)
+    def _():
+        low.wait_send()
+
+    @pl.when(has_before)
+    def _():
+        high.wait_send()
 
 
 def local(raw_frames, step_index, partner, flat_field):

time: 13 us -> 11.1 us (0.85)
  the two profiles are of different devices: /device:TPU:0 before, /device:TPU:4 now
where the time goes in v5:
time: 11.1 us; the launch traced here: 11 us
  Pallas kernels  10.4 us (94%)
  local copies, waits for them, and re-layouts  0.62 us (6%)
    pallas_call x1, Pallas kernels, local(): pl.pallas_call(body, out_shape=jax.ShapeDtypeStruct((angles, det), jnp.bf...  10.4 us
    unnamed x1, local copies, waits for them, and re-layouts  0.62 us

profile of v5, /device:TPU:4, one launch (start us, length us, event | category | flops | bytes accessed | tf_op | source)
XLA Modules:
  0.0 11.0 jit_solution(16531901694057124939)
XLA Ops:
  0.0 10.4 %shard_map.55 = bf16[8,2048]{1,0:T(8,128)(2,1)S(1)} custom-call(bf16[1,8,8,2048]{3,2,1,0:T(8,128)(2,1)} %refs_0_.1, s32[1,8]{1,0:T(1,128)} %refs_1_.1, s32[8]{0:T(128)} %refs_2_.1, bf16[2,2048]{1,0:T(2,128)(2,1)} %bitcast.3, bf16[17,256,256]{2,1,0:T(8,128)(2,1)} %constant.2.clone.refs_4_), custom_call_target="tpu_custom_call" | custom-call | tf_op jit(solution)/shard_map/pallas_call | solution.py:260
  10.4 0.6 %copy.7 = bf16[8,1,2048]{2,0,1:T(8,128)(2,1)} copy(bf16[8,1,2048]{2,0,1:T(8,128)(2,1)S(1)} %bitcast.2) | data formatting | bytes 65536

commit v6 on v5

--- a/solution.py
+++ b/solution.py
@@ -36,8 +36,8 @@
 
 def kernel(
     angles, blocks_row, raw_hbm, step_hbm, partner_hbm, flat_hbm, table_hbm, out_ref,
-    raw, table, step_ref, partner_ref, flat_ref, corr, halo, smooth, recv, stage, mirror, ring,
-    local_sem, halo_send, halo_recv, send_sem, recv_sem,
+    raw, table, step_ref, partner_ref, flat_ref, corr, halo, partial, edge, part, extra, smooth, recv, stage, mirror, ring,
+    local_sem, halo_send, halo_recv, edge_send, extra_recv, send_sem, recv_sem,
 ):
     steps, rows, det = raw.shape
     chunks = det // LANES
@@ -53,27 +53,47 @@
         pl.semaphore_signal(barrier, inc=1, device_id={"angle": lax.rem(me + k, angles)})
 
     raw_copy = pltpu.make_async_copy(raw_hbm.at[0], raw, local_sem.at[0])
-    raw_copy.start()
     step_copy = pltpu.make_async_copy(step_hbm, step_ref, local_sem.at[2])
     step_copy.start()
+    raw_copy.start()
     has_before = row > 0
     has_after = row < blocks_row - 1
 
     loop(1, angles, greet)
 
-    @pl.when(has_after)
+    cross_after = has_after & (lax.rem(row, 2) == 1)
+    cross_before = has_before & (lax.rem(row, 2) == 0)
+    chip_after = has_after & (lax.rem(row, 2) == 0)
+    chip_before = has_before & (lax.rem(row, 2) == 1)
+    first_row = (me == 0) & cross_before
+    last_row = (me == angles - 1) & cross_after
+    merged = first_row | last_row
+
+    @pl.when(chip_after)
     def _():
         pl.semaphore_signal(barrier, inc=1, device_id={"row": after})
 
-    @pl.when(has_before)
+    @pl.when(chip_before)
     def _():
         pl.semaphore_signal(barrier, inc=1, device_id={"row": before})
 
-    @pl.when(row == 0)
+    @pl.when(first_row)
+    def _():
+        loop(0, angles, lambda a: pl.semaphore_signal(
+            barrier, inc=1, device_id={"angle": a, "row": before}
+        ))
+
+    @pl.when(last_row)
+    def _():
+        loop(0, angles, lambda a: pl.semaphore_signal(
+            barrier, inc=1, device_id={"angle": a, "row": after}
+        ))
+
+    @pl.when(jnp.logical_not(chip_before))
     def _():
         halo[0] = jnp.zeros_like(halo[0])
 
-    @pl.when(row == blocks_row - 1)
+    @pl.when(jnp.logical_not(chip_after))
     def _():
         halo[1] = jnp.zeros_like(halo[1])
 
@@ -110,10 +130,6 @@
 
     loop(0, rows // 8, correlate)
 
-    pl.semaphore_wait(
-        barrier, angles - 1 + has_before.astype(jnp.int32) + has_after.astype(jnp.int32)
-    )
-
     def halo_copy(side, first, target):
         return pltpu.make_async_remote_copy(
             src_ref=corr.at[:, pl.ds(first * chunks, chunks), :],
@@ -123,27 +139,43 @@
             device_id={"row": target},
         )
 
-    low = halo_copy(0, rows - 1, after)
-    high = halo_copy(1, 0, before)
-
-    @pl.when(has_after)
-    def _():
-        low.start()
-
-    @pl.when(has_before)
-    def _():
-        high.start()
-
     def line(q, i):
         at = i * chunks if isinstance(i, int) else pl.multiple_of(i * chunks, chunks)
         return corr[q, pl.ds(at, chunks), :]
 
+    def ratios(i, lower, upper):
+        values = [0.25 * lower(q) + 0.5 * line(q, i) + 0.25 * upper(q) for q in range(3)]
+        values = [v.astype(jnp.bfloat16).astype(jnp.float32) for v in values]
+        scale = steps / values[2]
+        for q in range(2):
+            smooth[i, q] = (values[q] * scale).astype(jnp.bfloat16)
+
     def interior(i):
-        for q in range(3):
-            value = 0.25 * line(q, i - 1) + 0.5 * line(q, i) + 0.25 * line(q, i + 1)
-            smooth[i, q] = value.astype(jnp.bfloat16)
+        ratios(i, lambda q: line(q, i - 1), lambda q: line(q, i + 1))
 
     loop(1, rows - 1, interior)
+
+    for q in range(3):
+        inner = (0.5 * line(q, 0) + 0.25 * line(q, 1), 0.25 * line(q, rows - 2) + 0.5 * line(q, rows - 1))
+        outer = (0.25 * line(q, rows - 1), 0.25 * line(q, 0))
+        for side in range(2):
+            partial[side, q] = inner[side].astype(jnp.bfloat16)
+            edge[side, q] = outer[side].astype(jnp.bfloat16)
+
+    pl.semaphore_wait(
+        barrier, angles - 1 + has_before.astype(jnp.int32) + has_after.astype(jnp.int32)
+    )
+
+    low = halo_copy(0, rows - 1, after)
+    high = halo_copy(1, 0, before)
+
+    @pl.when(chip_after)
+    def _():
+        low.start()
+
+    @pl.when(chip_before)
+    def _():
+        high.start()
 
     def row_copy(target):
         return pltpu.make_async_remote_copy(
@@ -159,26 +191,72 @@
         def _():
             row_copy(target).start()
 
-    @pl.when(has_before)
-    def _():
-        low.wait_recv()
-
-    for q in range(3):
-        value = 0.25 * halo[0, q] + 0.5 * line(q, 0) + 0.25 * line(q, 1)
-        smooth[0, q] = value.astype(jnp.bfloat16)
-    send(0)
+    def part_copy(side, source):
+        return pltpu.make_async_remote_copy(
+            src_ref=partial.at[side],
+            dst_ref=part.at[source],
+            send_sem=send_sem.at[(0, angles - 1)[side]],
+            recv_sem=recv_sem.at[source],
+            device_id={"angle": (0, angles - 1)[side]},
+        )
+
+    def edge_copy(side, source):
+        return pltpu.make_async_remote_copy(
+            src_ref=edge.at[side],
+            dst_ref=extra.at[source],
+            send_sem=edge_send.at[side],
+            recv_sem=extra_recv.at[source],
+            device_id=({"angle": 0, "row": after}, {"angle": angles - 1, "row": before})[side],
+        )
+
+    @pl.when(cross_before & (me != 0))
+    def _():
+        part_copy(0, me).start()
+
+    @pl.when(cross_after)
+    def _():
+        edge_copy(0, me).start()
+
+    @pl.when(jnp.logical_not(cross_before))
+    def _():
+        @pl.when(chip_before)
+        def _():
+            low.wait_recv()
+
+        ratios(0, lambda q: halo[0, q], lambda q: line(q, 1))
+        send(0)
+
+    @pl.when(cross_after & (me != angles - 1))
+    def _():
+        part_copy(1, me).start()
+
+    @pl.when(cross_before)
+    def _():
+        edge_copy(1, me).start()
+
     loop(1, angles - 1, send)
 
-    @pl.when(has_after)
-    def _():
-        high.wait_recv()
-
-    for q in range(3):
-        value = 0.25 * line(q, rows - 2) + 0.5 * line(q, rows - 1) + 0.25 * halo[1, q]
-        smooth[rows - 1, q] = value.astype(jnp.bfloat16)
-    send(angles - 1)
-
-    recv[me] = smooth[me]
+    @pl.when(jnp.logical_not(cross_after))
+    def _():
+        @pl.when(chip_after)
+        def _():
+            high.wait_recv()
+
+        ratios(rows - 1, lambda q: line(q, rows - 2), lambda q: halo[1, q])
+        send(angles - 1)
+
+    @pl.when(jnp.logical_not(merged))
+    def _():
+        recv[me] = smooth[me]
+
+    @pl.when(first_row)
+    def _():
+        part[me] = partial[0]
+
+    @pl.when(last_row)
+    def _():
+        part[me] = partial[1]
+
     table_copy.wait()
     partner_copy.wait()
     flat_copy.wait()
@@ -193,11 +271,27 @@
             device_id={"angle": source},
         ).wait_recv()
 
-    loop(1, angles, arrived)
+    def merge(a):
+        values = [part[a, q].astype(jnp.float32) + extra[a, q].astype(jnp.float32) for q in range(3)]
+        scale = steps / values[2]
+        for q in range(2):
+            recv[a, q] = (values[q] * scale).astype(jnp.bfloat16)
+
+    @pl.when(jnp.logical_not(merged))
+    def _():
+        loop(1, angles, arrived)
+
+    for side, here in enumerate((first_row, last_row)):
+        @pl.when(here)
+        def _():
+            loop(1, angles, lambda k: part_copy(side, lax.rem(me + k, angles)).wait_recv())
+            loop(0, angles, lambda a: edge_copy(side, a).wait_recv())
+            loop(0, angles, merge)
+
 
     def spread(a):
         other = partner_ref[a]
-        for q in range(3):
+        for q in range(2):
             at = a * chunks if isinstance(a, int) else pl.multiple_of(a * chunks, chunks)
             stage[q, pl.ds(at, chunks), :] = recv[a, q].astype(jnp.float32)
             stage[q, pl.ds(at + angles * chunks, chunks), :] = recv[other, q].astype(jnp.float32)
@@ -208,8 +302,8 @@
     flat_cos, flat_sin = flat[0:1], flat[1:2]
     for c in range(chunks):
         lanes = slice(c * LANES, (c + 1) * LANES)
-        part = [stage[q, pl.ds(c, 2 * angles, stride=chunks), :] for q in range(3)]
-        value = steps * (part[1] * flat_cos[:, lanes] - part[0] * flat_sin[:, lanes]) / part[2]
+        taken = [stage[q, pl.ds(c, 2 * angles, stride=chunks), :] for q in range(2)]
+        value = taken[1] * flat_cos[:, lanes] - taken[0] * flat_sin[:, lanes]
         dpc = value.astype(jnp.bfloat16).astype(jnp.float32)
         block = c // (WIDTH // LANES)
         at = (c % (WIDTH // LANES)) * LANES
@@ -234,16 +328,36 @@
             block * angles : (block + 1) * angles
         ].astype(jnp.bfloat16)
 
-    def sent(k):
-        row_copy(lax.rem(me + k, angles)).wait_send()
-
-    loop(1, angles, sent)
-
-    @pl.when(has_after)
+    def sent(target):
+        @pl.when(target != me)
+        def _():
+            row_copy(target).wait_send()
+
+    loop(1, angles - 1, sent)
+    for side, crossing in enumerate((cross_before, cross_after)):
+        target = (0, angles - 1)[side]
+
+        @pl.when(jnp.logical_not(crossing))
+        def _():
+            sent(target)
+
+        @pl.when(crossing & (me != target))
+        def _():
+            part_copy(side, me).wait_send()
+
+    @pl.when(cross_after)
+    def _():
+        edge_copy(0, me).wait_send()
+
+    @pl.when(cross_before)
+    def _():
+        edge_copy(1, me).wait_send()
+
+    @pl.when(chip_after)
     def _():
         low.wait_send()
 
-    @pl.when(has_before)
+    @pl.when(chip_before)
     def _():
         high.wait_send()
 
@@ -270,14 +384,20 @@
             pltpu.VMEM((2, det), jnp.bfloat16),
             pltpu.VMEM((3, rows * chunks, LANES), jnp.float32),
             pltpu.VMEM((2, 3, chunks, LANES), jnp.float32),
-            pltpu.VMEM((rows, 3, chunks, LANES), jnp.bfloat16),
+            pltpu.VMEM((2, 3, chunks, LANES), jnp.bfloat16),
+            pltpu.VMEM((2, 3, chunks, LANES), jnp.bfloat16),
             pltpu.VMEM((angles, 3, chunks, LANES), jnp.bfloat16),
-            pltpu.VMEM((3, 2 * angles * chunks, LANES), jnp.float32),
+            pltpu.VMEM((angles, 3, chunks, LANES), jnp.bfloat16),
+            pltpu.VMEM((rows, 2, chunks, LANES), jnp.bfloat16),
+            pltpu.VMEM((angles, 2, chunks, LANES), jnp.bfloat16),
+            pltpu.VMEM((2, 2 * angles * chunks, LANES), jnp.float32),
             pltpu.VMEM((own * angles, WIDTH), jnp.float32),
             pltpu.VMEM((3 * own * angles, WIDTH), jnp.float32),
             pltpu.SemaphoreType.DMA((5,)),
             pltpu.SemaphoreType.DMA((2,)),
             pltpu.SemaphoreType.DMA((2,)),
+            pltpu.SemaphoreType.DMA((2,)),
+            pltpu.SemaphoreType.DMA((angles,)),
             pltpu.SemaphoreType.DMA((angles,)),
             pltpu.SemaphoreType.DMA((angles,)),
         ],

time: 11.1 us -> 10.5 us (0.946)
  the two profiles are of different devices: /device:TPU:4 before, /device:TPU:0 now
where the time goes in v6:
time: 10.5 us; the launch traced here: 10.4 us
  Pallas kernels  9.76 us (93%)
  local copies, waits for them, and re-layouts  0.62 us (6%)
    pallas_call x1, Pallas kernels, local(): pl.pallas_call(body, out_shape=jax.ShapeDtypeStruct((angles, det), jnp.bf...  9.76 us
    unnamed x1, local copies, waits for them, and re-layouts  0.62 us

profile of v6, /device:TPU:0, one launch (start us, length us, event | category | flops | bytes accessed | tf_op | source)
XLA Modules:
  0.0 10.4 jit_solution(4892932707241044951)
XLA Ops:
  0.0 9.8 %shard_map.55 = bf16[8,2048]{1,0:T(8,128)(2,1)S(1)} custom-call(bf16[1,8,8,2048]{3,2,1,0:T(8,128)(2,1)} %refs_0_.1, s32[1,8]{1,0:T(1,128)} %refs_1_.1, s32[8]{0:T(128)} %refs_2_.1, bf16[2,2048]{1,0:T(2,128)(2,1)} %bitcast.3, bf16[17,256,256]{2,1,0:T(8,128)(2,1)} %constant.2.clone.refs_4_), custom_call_target="tpu_custom_call" | custom-call | tf_op jit(solution)/shard_map/pallas_call | solution.py:374
  9.8 0.6 %copy.7 = bf16[8,1,2048]{2,0,1:T(8,128)(2,1)} copy(bf16[8,1,2048]{2,0,1:T(8,128)(2,1)S(1)} %bitcast.2) | data formatting | bytes 65536

commit v7 on v6

--- a/solution.py
+++ b/solution.py
@@ -155,6 +155,14 @@
 
     loop(1, rows - 1, interior)
 
+    @pl.when(jnp.logical_not(has_before))
+    def _():
+        ratios(0, lambda q: halo[0, q], lambda q: line(q, 1))
+
+    @pl.when(jnp.logical_not(has_after))
+    def _():
+        ratios(rows - 1, lambda q: line(q, rows - 2), lambda q: halo[1, q])
+
     for q in range(3):
         inner = (0.5 * line(q, 0) + 0.25 * line(q, 1), 0.25 * line(q, rows - 2) + 0.5 * line(q, rows - 1))
         outer = (0.25 * line(q, rows - 1), 0.25 * line(q, 0))
@@ -222,8 +230,8 @@
         @pl.when(chip_before)
         def _():
             low.wait_recv()
-
-        ratios(0, lambda q: halo[0, q], lambda q: line(q, 1))
+            ratios(0, lambda q: halo[0, q], lambda q: line(q, 1))
+
         send(0)
 
     @pl.when(cross_after & (me != angles - 1))
@@ -241,8 +249,8 @@
         @pl.when(chip_after)
         def _():
             high.wait_recv()
-
-        ratios(rows - 1, lambda q: line(q, rows - 2), lambda q: halo[1, q])
+            ratios(rows - 1, lambda q: line(q, rows - 2), lambda q: halo[1, q])
+
         send(angles - 1)
 
     @pl.when(jnp.logical_not(merged))

time: 10.5 us -> 10.6 us (level)
  no operation moved by 1% of the time
where the time goes in v7:
time: 10.6 us; the launch traced here: 10.4 us
  Pallas kernels  9.78 us (92%)
  local copies, waits for them, and re-layouts  0.62 us (6%)
    pallas_call x1, Pallas kernels, local(): pl.pallas_call(body, out_shape=jax.ShapeDtypeStruct((angles, det), jnp.bf...  9.78 us
    unnamed x1, local copies, waits for them, and re-layouts  0.62 us

profile of v7, /device:TPU:0, one launch (start us, length us, event | category | flops | bytes accessed | tf_op | source)
XLA Modules:
  0.0 10.4 jit_solution(15136021647551930703)
XLA Ops:
  0.0 9.8 %shard_map.55 = bf16[8,2048]{1,0:T(8,128)(2,1)S(1)} custom-call(bf16[1,8,8,2048]{3,2,1,0:T(8,128)(2,1)} %refs_0_.1, s32[1,8]{1,0:T(1,128)} %refs_1_.1, s32[8]{0:T(128)} %refs_2_.1, bf16[2,2048]{1,0:T(2,128)(2,1)} %bitcast.3, bf16[17,256,256]{2,1,0:T(8,128)(2,1)} %constant.2.clone.refs_4_), custom_call_target="tpu_custom_call" | custom-call | tf_op jit(solution)/shard_map/pallas_call | solution.py:382
  9.8 0.6 %copy.7 = bf16[8,1,2048]{2,0,1:T(8,128)(2,1)} copy(bf16[8,1,2048]{2,0,1:T(8,128)(2,1)S(1)} %bitcast.2) | data formatting | bytes 65536
